TPU v7x, 32 devices: a whole 2x2x4 slice. The times are simulated.
32 devices in a mesh: groups: 2 (over y), ctx: 4 (over z), tp: 4 (over x, core).
Axes of the slice: x: 2, y: 2, z: 4, core: 2. Of those that a mesh axis runs over, the one named last changes fastest.
Arguments:
- queries: bfloat16 [2048, 5120], P(('groups', 'ctx'), 'tp'), parts along dimension 0, may hold values from -16 to 16
- keys: bfloat16 [2048, 1024], P(('groups', 'ctx'), 'tp'), parts along dimension 0, may hold values from -16 to 16
- values: bfloat16 [2048, 1024], P(('groups', 'ctx'), 'tp'), parts along dimension 0, may hold values from -6 to 6
- positions: int32 [2048], P('groups'), parts along dimension 0, may hold values from 0 to 1023, as said below
- out_weight: bfloat16 [5120, 5120], P('tp', 'ctx'), may hold values from -0.59765625 to 0.59765625
Outputs:
- mixed: bfloat16 [2048, 5120], P(('groups', 'ctx'), 'tp'), parts along dimension 0
There are 2 independent parts, one for each index of `groups`. A program takes and returns all parts, laid end to end along the dimension named above; an argument that names none is the same for every part. Nothing has to cross between parts.
Inputs may be any that keep to these rules, and one draw needn't show every extreme that they name: positions is a permutation of all positions made of 8 aligned runs of 128 consecutive positions, each run increasing.
All inputs are finite; a program needn't handle non-finite values.
Results may differ from a plain program's by a relative error of at most 0.0095.
Values may be sent and summed in bfloat16 or wider, within the bound.
No kernel may reach another device: no remote copies, remote signals or barrier semaphores. Data moves between devices by JAX's collectives and lax.ppermute only.
A program may use at most 64 MiB of HBM per device.

v0:
```python
import math
import jax
import jax.numpy as jnp
from jax import lax
from jax.sharding import PartitionSpec as P

QUERY_HEADS = 40
KEY_VALUE_HEADS = 8
HEAD_SIZE = 128


def local(queries, keys, values, positions, out_weight):
    tok = queries.shape[0]
    kv_heads = keys.shape[1] // HEAD_SIZE
    query_group = QUERY_HEADS // KEY_VALUE_HEADS
    scale = HEAD_SIZE ** (-0.5)
    ctx_index = lax.axis_index("ctx")
    query_pos = lax.dynamic_slice_in_dim(positions, ctx_index * tok, tok)
    query_four = queries.reshape(tok, kv_heads, query_group, HEAD_SIZE)

    def attend(carry, key_block, value_block, key_pos):
        top, total, accum = carry
        count = key_block.shape[0]
        key_three = key_block.reshape(count, kv_heads, HEAD_SIZE)
        value_three = value_block.reshape(count, kv_heads, HEAD_SIZE)
        scores = (
            jnp.einsum("tgjd,kgd->gjtk", query_four, key_three, preferred_element_type=jnp.float32)
            * scale
        )
        keep = key_pos[None, :] <= query_pos[:, None]
        scores = jnp.where(keep, scores, -1e30)
        new_top = jnp.maximum(top, jnp.max(scores, axis=-1))
        factor = jnp.exp(top - new_top)
        expo = jnp.where(keep, jnp.exp(scores - new_top[..., None]), 0.0)
        total = total * factor + jnp.sum(expo, axis=-1)
        weights = expo.astype(jnp.bfloat16)
        accum = accum * factor[..., None] + jnp.einsum(
            "gjtk,kgd->gjtd", weights, value_three, preferred_element_type=jnp.float32
        )
        return (new_top, total, accum)

    start_top = jnp.full((kv_heads, query_group, tok), -1e30, jnp.float32)
    start_total = jnp.zeros((kv_heads, query_group, tok), jnp.float32)
    start_accum = jnp.zeros((kv_heads, query_group, tok, HEAD_SIZE), jnp.float32)
    key_piece = lax.all_gather(keys, "ctx", axis=0, tiled=True)
    value_piece = lax.all_gather(values, "ctx", axis=0, tiled=True)
    rows = key_piece.shape[0]
    width = math.gcd(rows, 512)

    def step(index, state):
        offset = index * width
        key_block = lax.dynamic_slice_in_dim(key_piece, offset, width, 0)
        value_block = lax.dynamic_slice_in_dim(value_piece, offset, width, 0)
        key_pos = lax.dynamic_slice_in_dim(positions, offset, width, 0)
        return attend(state, key_block, value_block, key_pos)

    top, total, accum = lax.fori_loop(0, rows // width, step, (start_top, start_total, start_accum))
    attended = (
        (accum / total[..., None])
        .transpose(2, 0, 1, 3)
        .reshape(tok, kv_heads * query_group * HEAD_SIZE)
        .astype(jnp.bfloat16)
    )
    partial_value = jnp.dot(
        attended,
        lax.all_gather(out_weight, "ctx", axis=1, tiled=True),
        preferred_element_type=jnp.float32,
    )
    summed = lax.psum_scatter(
        partial_value.astype(jnp.bfloat16), "tp", scatter_dimension=1, tiled=True
    )
    return summed


def solution(mesh):
    return jax.shard_map(
        local,
        mesh=mesh,
        in_specs=(
            P(("groups", "ctx"), "tp"),
            P(("groups", "ctx"), "tp"),
            P(("groups", "ctx"), "tp"),
            P("groups"),
            P("tp", "ctx"),
        ),
        out_specs=P(("groups", "ctx"), "tp"),
        check_vma=False,
    )
```

profile of v0, /device:TPU:0, one launch (start us, length us, event | category | flops | bytes accessed | tf_op | source)
XLA Modules:
  0.0 296.8 jit_solution(16109879064267613819)
XLA Ops:
  6.5 0.0 all-gather.2.cloned.1.call-start
  6.5 0.7 all-gather.2.cloned.1.call-update
  7.3 0.0 reduce-scatter.2.cloned.1.call-start
  7.3 1.3 copy.11
  8.7 0.3 copy.13
  9.0 0.0 copy-done.1
  9.0 0.1 copy.12
  9.1 0.0 copy-done.2
  9.1 0.1 copy.10
  9.2 0.0 copy-done.3
  9.2 0.1 dynamic_slice.24
  9.3 19.1 %all_gather.10 = bf16[1024,256]{0,1:T(8,128)(2,1)S(1)} all-gather(bf16[256,256]{0,1:T(8,128)(2,1)S(1)} %copy.12), channel_id=1, replica_groups=mesh['groups'=2,'ctx'=4,'tp'=4] {'ctx'}, dimensions={0}, use_global_device_ids=true | all-gather | bytes 655360 | tf_op jit(solution)/shard_map/all_gather | solution.py:46
  28.4 30.9 %all_gather.9 = bf16[1024,256]{0,1:T(8,128)(2,1)S(1)} all-gather(bf16[256,256]{0,1:T(8,128)(2,1)S(1)} %copy.10), channel_id=1, replica_groups=mesh['groups'=2,'ctx'=4,'tp'=4] {'ctx'}, dimensions={0}, use_global_device_ids=true | all-gather | bytes 655360 | tf_op jit(solution)/shard_map/all_gather | solution.py:45
  59.3 19.9 %while.18 = (s32[]{:T(128)}, f32[2,5,256]{2,1,0:T(8,128)S(1)}, f32[2,5,256]{2,1,0:T(8,128)S(1)}, f32[2,5,256,128]{3,2,1,0:T(8,128)S(1)}, s32[1024]{0:T(1024)S(1)...) while((s32[]{:T(128)}, f32[2,5,256]{2,1,0:T(8,128)S(1)}, ...), condition=%wide.region_3.4_spmd.clone, body=%wide.region_0.3_spmd.clone.sunk | while | flops 689254912 | bytes 42245336 | solution.py:57
  59.3 0.1 dynamic_slice.33
  59.3 0.1 broadcast_compare_fusion.2
  59.6 3.3 %fusion.30 = (f32[2,5,256]{2,1,0:T(8,128)S(1)}, f32[2,512,256,5]{2,1,3,0:T(8,128)}) fusion(pred[256,512]{0,1:T(8,128)(4,1)S(1)} %broadcast_compare_fusion.2, bf16[512,2,128,1]{0,2,3,1:T(8,128)(2,1)S(1)} %bitcast.48, bf16[256,2,5,128]{3,0,2,1:T(8,128)(2,1)S(1)} %get-tuple-element.325), kind=kOutput, calls=%fused_computation.2.clone.1 | convolution fusion | flops 339473920 | bytes 6301696 | tf_op jit(solution)/shard_map/while/body/eval_jaxpr/tgjd,kgd->gjtk/dot_general | solution.py:27
  62.9 4.0 %fusion.31 = f32[2,5,256]{2,1,0:T(8,128)S(1)} fusion(f32[2,512,256,5]{2,1,3,0:T(8,128)} %get-tuple-element.288, f32[2,5,256]{2,1,0:T(8,128)S(1)} %select_maximum_fusion.2, pred[256,512]{0,1:T(8,128)(4,1)S(1)} %broadcast_compare_fusion.2), kind=kLoop, calls=%fused_computation.4.clone.1 | loop fusion | flops 6551040 | bytes 5394432 | tf_op jit(solution)/shard_map/while/body/eval_jaxpr/reduce_sum | solution.py:35
  66.9 0.2 copy-done
  67.1 2.2 fusion.33
  69.3 0.1 dynamic_slice.33
  69.4 0.1 broadcast_compare_fusion.2
  69.6 3.3 %fusion.30 = (f32[2,5,256]{2,1,0:T(8,128)S(1)}, f32[2,512,256,5]{2,1,3,0:T(8,128)}) fusion(pred[256,512]{0,1:T(8,128)(4,1)S(1)} %broadcast_compare_fusion.2, bf16[512,2,128,1]{0,2,3,1:T(8,128)(2,1)S(1)} %bitcast.48, bf16[256,2,5,128]{3,0,2,1:T(8,128)(2,1)S(1)} %get-tuple-element.325), kind=kOutput, calls=%fused_computation.2.clone.1 | convolution fusion | flops 339473920 | bytes 6301696 | tf_op jit(solution)/shard_map/while/body/eval_jaxpr/tgjd,kgd->gjtk/dot_general | solution.py:27
  72.9 3.9 %fusion.31 = f32[2,5,256]{2,1,0:T(8,128)S(1)} fusion(f32[2,512,256,5]{2,1,3,0:T(8,128)} %get-tuple-element.288, f32[2,5,256]{2,1,0:T(8,128)S(1)} %select_maximum_fusion.2, pred[256,512]{0,1:T(8,128)(4,1)S(1)} %broadcast_compare_fusion.2), kind=kLoop, calls=%fused_computation.4.clone.1 | loop fusion | flops 6551040 | bytes 5394432 | tf_op jit(solution)/shard_map/while/body/eval_jaxpr/reduce_sum | solution.py:35
  76.8 0.1 copy-done
  77.0 2.2 fusion.33
  79.2 0.4 copy.14
  79.6 0.1 divide_convert_fusion
  79.8 167.2 %all-gather.2.cloned.1.call-done = bf16[1280,5120]{1,0:T(8,128)(2,1)} async-done(((bf16[1280,1280]{1,0:T(8,128)(2,1)}), bf16[1280,5120]{1,0:T(8,128)(2,1)}) %all-gather.2.cloned.1.call-update) | async-done | bytes 13107216 | tf_op jit(solution)/shard_map/all_gather | solution.py:66
  247.0 9.7 %convolution_convert_fusion = bf16[256,5120]{1,0:T(8,128)(2,1)} fusion(bf16[256,1280]{0,1:T(8,128)(2,1)S(1)} %bitcast.50, bf16[1280,5120]{1,0:T(8,128)(2,1)} %all-gather.2.cloned.1.call-done), kind=kOutput, calls=%fused_computation.19 | convolution fusion | flops 3356753920 | bytes 16384000 | tf_op jit(solution)/shard_map/dot_general | solution.py:64
  256.7 0.0 reduce-scatter.2.cloned.1.call-update
  256.7 33.3 %reduce-scatter.2.cloned.1.call-done = bf16[256,1280]{1,0:T(8,128)(2,1)} async-done(((bf16[256,5120]{1,0:T(8,128)(2,1)}), bf16[256,1280]{1,0:T(8,128)(2,1)}) %reduce-scatter.2.cloned.1.call-update) | async-done | bytes 655376 | tf_op jit(solution)/shard_map/reduce_scatter | solution.py:69
  (16 shorter events, 0.2 us)
Async XLA Ops:
  6.5 2.5 copy-start.1
  6.5 2.6 copy-start.2
  6.5 2.7 copy-start.3
  6.5 240.4 %all-gather.2.cloned.1.call-start = ((), (), s32[]{:S(2)}) async-start(), calls=%async_computation.1 | async-start | bytes 16384000 | tf_op jit(solution)/shard_map/all_gather | solution.py:66
  7.3 282.7 %reduce-scatter.2.cloned.1.call-start = ((), (), s32[]{:S(2)}) async-start(), calls=%async_computation.2 | async-start | bytes 3276800 | tf_op jit(solution)/shard_map/reduce_scatter | solution.py:69
  62.9 4.2 %copy-start = (f32[2,512,256,5]{2,1,3,0:T(8,128)S(1)}, f32[2,512,256,5]{2,1,3,0:T(8,128)}, u32[]{:S(2)}) copy-start(f32[2,512,256,5]{2,1,3,0:T(8,128)} %get-tuple-element.288) | copy-start | bytes 15728644 | tf_op jit(solution)/shard_map/while
  72.9 4.0 %copy-start = (f32[2,512,256,5]{2,1,3,0:T(8,128)S(1)}, f32[2,512,256,5]{2,1,3,0:T(8,128)}, u32[]{:S(2)}) copy-start(f32[2,512,256,5]{2,1,3,0:T(8,128)} %get-tuple-element.288) | copy-start | bytes 15728644 | tf_op jit(solution)/shard_map/while
Sparse Core Ops, SparseCore 0:
  8.9 238.0 all-gather.1
  256.8 33.1 reduce-scatter.1
where the time goes:
time: 297 us
  waiting for transfers between devices  201 us (68%)
  blocking collectives  49.9 us (17%)
  matrix products  20.8 us (7%)
  between operations  13.5 us (5%)
  other arithmetic  8.32 us (3%)
    all_gather x1, waiting for transfers between devices, local(): lax.all_gather(out_weight, 'ctx', axis=1, tiled=True)  167 us
    reduce_scatter x1, waiting for transfers between devices, local(): lax.psum_scatter(partial_value.astype(jnp.bfloat16), 'tp', scatter_dimens...  33.3 us
    all_gather x1, blocking collectives, local(): key_piece = lax.all_gather(keys, 'ctx', axis=0, tiled=True)  30.9 us
    all_gather x1, blocking collectives, local(): value_piece = lax.all_gather(values, 'ctx', axis=0, tiled=True)  19.1 us
    dot_general x1, matrix products, local(): jnp.dot(attended, lax.all_gather(out_weight, 'ctx', axis=1, tiled=True),...  9.69 us
    reduce_sum x2, other arithmetic, attend(): total = total * factor + jnp.sum(expo, axis=-1)  7.85 us
    dot_general x2, matrix products, attend(): jnp.einsum('tgjd,kgd->gjtk', query_four, key_three, preferred_element_typ...  6.64 us
  transfers between devices with their start and end apart: 2, of which 2 were waited for; matrix products, arithmetic and copies ran while one was open for 7% of the time, Pallas kernels for 0%

commit v1 on v0

--- a/solution.py
+++ b/solution.py
@@ -42,8 +42,11 @@
     start_top = jnp.full((kv_heads, query_group, tok), -1e30, jnp.float32)
     start_total = jnp.zeros((kv_heads, query_group, tok), jnp.float32)
     start_accum = jnp.zeros((kv_heads, query_group, tok, HEAD_SIZE), jnp.float32)
-    key_piece = lax.all_gather(keys, "ctx", axis=0, tiled=True)
-    value_piece = lax.all_gather(values, "ctx", axis=0, tiled=True)
+    key_piece, value_piece = jnp.split(
+        lax.all_gather(jnp.concatenate([keys, values], 1), axis_name="ctx", axis=0, tiled=True),
+        [keys.shape[1]],
+        1,
+    )
     rows = key_piece.shape[0]
     width = math.gcd(rows, 512)
 

time: 297 us -> 318 us (1.071)
  waiting for transfers between devices: 201 us -> 267 us
  blocking collectives: 49.9 us -> 0 us
  local copies, waits for them, and re-layouts: 2.89 us -> 6.76 us
    all_gather x2 -> x0, blocking collectives: 49.9 us -> none  [the longest x1 30.9 us: local(): key_piece = lax.all_gather(keys, 'ctx', axis=0, tiled=True)]
    all_gather x1, waiting for transfers between devices: 167 us -> 203 us  [local(): lax.all_gather(out_weight, 'ctx', axis=1, tiled=True)]
    all_gather x0 -> x1, waiting for transfers between devices: none -> 30.2 us  [local(): lax.all_gather(jnp.concatenate([keys, values], 1), axis_name='ctx', axis=...]
  transfers between devices with their start and end apart: 2 -> 3, of which waited for: 2 -> 3; matrix products, arithmetic and copies ran while one was open for 7% -> 7% of each run, Pallas kernels for 0% -> 0%
where the time goes in v1:
time: 318 us
  waiting for transfers between devices  267 us (84%)
  matrix products  20.7 us (7%)
  between operations  13.2 us (4%)
  other arithmetic  9.68 us (3%)
  local copies, waits for them, and re-layouts  6.76 us (2%)
    all_gather x1, waiting for transfers between devices, local(): lax.all_gather(out_weight, 'ctx', axis=1, tiled=True)  203 us
    reduce_scatter x1, waiting for transfers between devices, local(): lax.psum_scatter(partial_value.astype(jnp.bfloat16), 'tp', scatter_dimens...  32.7 us
    all_gather x1, waiting for transfers between devices, local(): lax.all_gather(jnp.concatenate([keys, values], 1), axis_name='ctx', axis=...  30.2 us
    dot_general x1, matrix products, local(): jnp.dot(attended, lax.all_gather(out_weight, 'ctx', axis=1, tiled=True),...  9.67 us
    reduce_sum x2, other arithmetic, attend(): total = total * factor + jnp.sum(expo, axis=-1)  8.5 us
    dot_general x2, matrix products, attend(): jnp.einsum('tgjd,kgd->gjtk', query_four, key_three, preferred_element_typ...  6.62 us
  transfers between devices with their start and end apart: 3, of which 3 were waited for; matrix products, arithmetic and copies ran while one was open for 7% of the time, Pallas kernels for 0%

profile of v1, /device:TPU:0, one launch (start us, length us, event | category | flops | bytes accessed | tf_op | source)
XLA Modules:
  0.0 317.7 jit_solution(3241197346551124525)
XLA Ops:
  6.5 0.0 all-gather.3.cloned.1.call-start
  6.5 1.0 copy.10
  7.6 1.0 copy.11
  8.6 0.7 pad_maximum_fusion
  9.3 0.0 all-gather.3.cloned.1.call-update
  9.3 0.0 all-gather.5.cloned.1.call-start
  9.4 0.7 all-gather.5.cloned.1.call-update
  10.1 0.0 reduce-scatter.2.cloned.1.call-start
  10.2 1.3 copy.12
  11.5 0.3 copy.13
  11.8 0.1 dynamic_slice.24
  11.9 30.2 %all-gather.3.cloned.1.call-done = bf16[1024,512]{0,1:T(8,128)(2,1)} async-done(((bf16[256,512]{0,1:T(8,128)(2,1)}), bf16[1024,512]{0,1:T(8,128)(2,1)}) %all-gather.3.cloned.1.call-update) | async-done | bytes 1048592 | tf_op jit(solution)/shard_map/all_gather | solution.py:46
  42.1 1.3 fusion.13
  43.4 21.4 %while.18 = (s32[]{:T(128)}, f32[2,5,256]{2,1,0:T(8,128)S(1)}, f32[2,5,256]{2,1,0:T(8,128)S(1)}, f32[2,5,256,128]{3,2,1,0:T(8,128)S(1)}, s32[1024]{0:T(1024)S(1)...) while((s32[]{:T(128)}, f32[2,5,256]{2,1,0:T(8,128)S(1)}, ...), condition=%wide.region_3.4_spmd.clone, body=%wide.region_0.3_spmd.clone.sunk | while | flops 689254912 | bytes 42245336 | solution.py:60
  43.4 0.1 dynamic_slice.33
  43.5 0.1 broadcast_compare_fusion.2
  43.7 3.3 %fusion.31 = (f32[2,5,256]{2,1,0:T(8,128)S(1)}, f32[2,512,256,5]{2,1,3,0:T(8,128)}) fusion(pred[256,512]{0,1:T(8,128)(4,1)S(1)} %broadcast_compare_fusion.2, bf16[512,2,128,1]{0,2,3,1:T(8,128)(2,1)S(1)} %bitcast.48, bf16[256,2,5,128]{3,0,2,1:T(8,128)(2,1)S(1)} %get-tuple-element.327), kind=kOutput, calls=%fused_computation.2.clone.1 | convolution fusion | flops 339473920 | bytes 6301696 | tf_op jit(solution)/shard_map/while/body/eval_jaxpr/tgjd,kgd->gjtk/dot_general | solution.py:27
  47.0 4.5 %fusion.32 = f32[2,5,256]{2,1,0:T(8,128)S(1)} fusion(f32[2,512,256,5]{2,1,3,0:T(8,128)} %get-tuple-element.290, f32[2,5,256]{2,1,0:T(8,128)S(1)} %select_maximum_fusion.2, pred[256,512]{0,1:T(8,128)(4,1)S(1)} %broadcast_compare_fusion.2), kind=kLoop, calls=%fused_computation.4.clone.1 | loop fusion | flops 6551040 | bytes 5394432 | tf_op jit(solution)/shard_map/while/body/eval_jaxpr/reduce_sum | solution.py:35
  51.6 0.9 copy-done
  52.5 2.2 fusion.34
  54.7 0.1 dynamic_slice.33
  54.8 0.1 broadcast_compare_fusion.2
  55.0 3.3 %fusion.31 = (f32[2,5,256]{2,1,0:T(8,128)S(1)}, f32[2,512,256,5]{2,1,3,0:T(8,128)}) fusion(pred[256,512]{0,1:T(8,128)(4,1)S(1)} %broadcast_compare_fusion.2, bf16[512,2,128,1]{0,2,3,1:T(8,128)(2,1)S(1)} %bitcast.48, bf16[256,2,5,128]{3,0,2,1:T(8,128)(2,1)S(1)} %get-tuple-element.327), kind=kOutput, calls=%fused_computation.2.clone.1 | convolution fusion | flops 339473920 | bytes 6301696 | tf_op jit(solution)/shard_map/while/body/eval_jaxpr/tgjd,kgd->gjtk/dot_general | solution.py:27
  58.4 4.0 %fusion.32 = f32[2,5,256]{2,1,0:T(8,128)S(1)} fusion(f32[2,512,256,5]{2,1,3,0:T(8,128)} %get-tuple-element.290, f32[2,5,256]{2,1,0:T(8,128)S(1)} %select_maximum_fusion.2, pred[256,512]{0,1:T(8,128)(4,1)S(1)} %broadcast_compare_fusion.2), kind=kLoop, calls=%fused_computation.4.clone.1 | loop fusion | flops 6551040 | bytes 5394432 | tf_op jit(solution)/shard_map/while/body/eval_jaxpr/reduce_sum | solution.py:35
  62.4 0.2 copy-done
  62.5 2.2 fusion.34
  64.8 0.4 copy.14
  65.2 0.1 divide_convert_fusion
  65.3 203.5 %all-gather.5.cloned.1.call-done = bf16[1280,5120]{1,0:T(8,128)(2,1)} async-done(((bf16[1280,1280]{1,0:T(8,128)(2,1)}), bf16[1280,5120]{1,0:T(8,128)(2,1)}) %all-gather.5.cloned.1.call-update) | async-done | bytes 13107216 | tf_op jit(solution)/shard_map/all_gather | solution.py:69
  268.8 9.7 %convolution_convert_fusion = bf16[256,5120]{1,0:T(8,128)(2,1)} fusion(bf16[256,1280]{0,1:T(8,128)(2,1)S(1)} %bitcast.50, bf16[1280,5120]{1,0:T(8,128)(2,1)} %all-gather.5.cloned.1.call-done), kind=kOutput, calls=%fused_computation.19 | convolution fusion | flops 3356753920 | bytes 16384000 | tf_op jit(solution)/shard_map/dot_general | solution.py:67
  278.4 0.0 reduce-scatter.2.cloned.1.call-update
  278.5 32.7 %reduce-scatter.2.cloned.1.call-done = bf16[256,1280]{1,0:T(8,128)(2,1)} async-done(((bf16[256,5120]{1,0:T(8,128)(2,1)}), bf16[256,1280]{1,0:T(8,128)(2,1)}) %reduce-scatter.2.cloned.1.call-update) | async-done | bytes 655376 | tf_op jit(solution)/shard_map/reduce_scatter | solution.py:72
  (15 shorter events, 0.1 us)
Async XLA Ops:
  6.5 5.3 %copy-start.1 = (s32[1024]{0:T(1024)S(1)}, s32[1024]{0:T(1024)}, u32[]{:S(2)}) copy-start(s32[1024]{0:T(1024)} %param.10) | copy-start | bytes 12292
  6.5 35.6 %all-gather.3.cloned.1.call-start = ((), (), s32[]{:S(2)}) async-start(), calls=%async_computation.1 | async-start | bytes 1310720 | tf_op jit(solution)/shard_map/all_gather | solution.py:46
  9.3 259.5 %all-gather.5.cloned.1.call-start = ((), (), s32[]{:S(2)}) async-start(), calls=%async_computation.2 | async-start | bytes 16384000 | tf_op jit(solution)/shard_map/all_gather | solution.py:69
  10.1 301.1 %reduce-scatter.2.cloned.1.call-start = ((), (), s32[]{:S(2)}) async-start(), calls=%async_computation.3 | async-start | bytes 3276800 | tf_op jit(solution)/shard_map/reduce_scatter | solution.py:72
  47.0 5.5 %copy-start = (f32[2,512,256,5]{2,1,3,0:T(8,128)S(1)}, f32[2,512,256,5]{2,1,3,0:T(8,128)}, u32[]{:S(2)}) copy-start(f32[2,512,256,5]{2,1,3,0:T(8,128)} %get-tuple-element.290) | copy-start | bytes 15728644 | tf_op jit(solution)/shard_map/while
  58.3 4.2 %copy-start = (f32[2,512,256,5]{2,1,3,0:T(8,128)S(1)}, f32[2,512,256,5]{2,1,3,0:T(8,128)}, u32[]{:S(2)}) copy-start(f32[2,512,256,5]{2,1,3,0:T(8,128)} %get-tuple-element.290) | copy-start | bytes 15728644 | tf_op jit(solution)/shard_map/while
Sparse Core Ops, SparseCore 0:
  9.4 32.6 all-gather.2
  43.7 225.0 all-gather.4
  278.6 32.5 reduce-scatter.1
